TPU v7x, 256 devices: a whole 4x4x8 slice. The times are simulated.
256 devices in a mesh: pair: 64 (over x_hi, z, y), sigma: 4 (over x_lo, core).
Axes of the slice: x: 4 (x_hi: 2, x_lo: 2; x = x_hi * 2 + x_lo), y: 4, z: 8, core: 2. Of those that a mesh axis runs over, the one named last changes fastest.
Arguments:
- pair_density_matrices: bfloat16 [131072, 1536], P('pair'), may hold values from -16 to 16
- energy_bins: int32 [131072, 2], P('pair'), may hold values from 0 to 63
- bin_weights: float32 [2, 64], replicated, may hold values from 0.05 to 1
- coulomb: float32 [1536], replicated, may hold values from 0.5 to 4
- state_matrices: bfloat16 [1536, 2048], P(None, 'sigma'), may hold values from -6 to 6
Outputs:
- screened_states: float32 [1536, 2, 2048], P('pair', None, 'sigma')
- sigma_diag: float32 [2, 2048], P(None, 'sigma')
All inputs are finite; a program needn't handle non-finite values.
Results may differ from a plain program's by a relative error of at most 0.00035.
Values sent between devices are 32-bit elements; how exact they have to be, the bound alone decides.
No kernel may reach another device: no remote copies, remote signals or barrier semaphores. Data moves between devices by JAX's collectives and lax.ppermute only.
A program may use at most 64 MiB of HBM per device.

v0:
```python
import jax
import jax.numpy as jnp
from jax import lax
from jax.sharding import PartitionSpec as P


def pair_weights(energy_bins, bin_weights, pair_total):
    bin_levels = jnp.arange(bin_weights.shape[1], dtype=jnp.int32)
    matches = (energy_bins[:, :, None] == bin_levels[None, None, :]).astype(jnp.float32)
    picked = jnp.sum(matches * bin_weights[None, :, :], axis=2)
    return picked.T / jnp.float32(pair_total)


def local(pair_density_matrices, energy_bins, bin_weights, coulomb, state_matrices):
    pair_local, width = pair_density_matrices.shape
    pair_count = lax.axis_size("pair")
    self_energy_count = lax.axis_size("sigma")
    row_count = width // pair_count
    col_count = width // self_energy_count
    pair_position = lax.axis_index("pair")
    sigma_pos = lax.axis_index("sigma")
    weight = pair_weights(energy_bins, bin_weights, pair_local * pair_count)
    column_slab = lax.dynamic_slice_in_dim(
        pair_density_matrices, sigma_pos * col_count, col_count, 1
    )
    scaled_product = (weight[:, :, None] * column_slab[None, :, :].astype(jnp.float32)).astype(
        jnp.bfloat16
    )
    polar_block = lax.psum_scatter(
        -jnp.einsum(
            "zh,vzo->hvo", pair_density_matrices, scaled_product, preferred_element_type=jnp.float32
        ),
        "pair",
        scatter_dimension=0,
        tiled=True,
    )
    coulomb_root = jnp.sqrt(coulomb)
    root_rows = lax.dynamic_slice_in_dim(coulomb_root, pair_position * row_count, row_count, 0)
    coulomb_root_columns = lax.dynamic_slice_in_dim(
        coulomb_root, sigma_pos * col_count, col_count, 0
    )
    screened = root_rows[:, None, None] * polar_block * coulomb_root_columns[None, None, :]
    states_wide = state_matrices.astype(jnp.float32)
    applied = jnp.einsum(
        "rfc,cn->rfn",
        lax.all_gather(screened, "sigma", axis=2, tiled=True),
        states_wide,
        precision=lax.Precision.HIGHEST,
    )
    own_states = lax.dynamic_slice_in_dim(states_wide, pair_position * row_count, row_count, 0)
    partial_contribution = jnp.sum(own_states[:, None, :] * applied, axis=0) / jnp.float32(width)
    sigma_diag = lax.psum(partial_contribution, "pair")
    return (applied, sigma_diag)


def solution(mesh):
    return jax.shard_map(
        local,
        mesh=mesh,
        in_specs=(P("pair", None), P("pair", None), P(), P(), P(None, "sigma")),
        out_specs=(P("pair", None, "sigma"), P(None, "sigma")),
        check_vma=False,
    )
```

profile of v0, /device:TPU:2, one launch (start us, length us, event | category | flops | bytes accessed | tf_op | source)
XLA Modules:
  0.0 1032.7 jit_solution(59104497414728657)
XLA Ops:
  7.2 0.0 reduce-scatter.2.cloned.1.call-start
  7.2 1.0 select_reduce_fusion
  8.2 1.6 dynamic-slice_convert_fusion
  9.9 10.4 %negate_bitcast_fusion = f32[1536,2,384]{2,0,1:T(8,128)} fusion(bf16[2048,1536]{1,0:T(8,128)(2,1)} %param.5, f32[2048,384]{1,0:T(8,128)S(1)} %dynamic-slice_convert_fusion, f32[2,2048]{1,0:T(2,128)S(1)} %multiply_bitcast_fusion), kind=kOutput, calls=%fused_computation.3 | convolution fusion | flops 4836163584 | bytes 14172160 | tf_op jit(solution)/shard_map/zh,vzo->hvo/dot_general | solution.py:30
  20.3 0.0 copy-start.1
  20.3 0.0 copy-start
  20.3 0.0 reduce-scatter.2.cloned.1.call-update
  20.3 0.7 copy-done.1
  21.0 0.1 dynamic_slice.14
  21.1 0.1 dynamic_slice.12
  21.2 0.6 copy-done
  21.7 814.2 %reduce-scatter.2.cloned.1.call-done = f32[24,2,384]{2,0,1:T(8,128)} async-done(((f32[1536,2,384]{2,0,1:T(8,128)}), f32[24,2,384]{2,0,1:T(8,128)}) %reduce-scatter.2.cloned.1.call-update) | async-done | bytes 73744 | tf_op jit(solution)/shard_map/reduce_scatter | solution.py:29
  836.0 1.0 multiply_multiply_fusion
  836.9 5.9 all_gather.3
  842.8 0.9 multiply_reduce_fusion
  843.7 0.7 copy.10
  844.4 181.4 %psum.7 = f32[2,512]{1,0:T(2,128)} all-reduce(f32[2,512]{1,0:T(2,128)S(1)} %broadcast_multiply_fusion), channel_id=1, replica_groups=mesh['pair'=64,'sigma'=4] {'pair'}, use_global_device_ids=true, to_apply=%region_3.0 | all-reduce | flops 1024 | bytes 8192 | tf_op jit(solution)/shard_map/psum | solution.py:52
  (4 shorter events, 0.0 us)
Async XLA Ops:
  7.2 828.8 %reduce-scatter.2.cloned.1.call-start = ((), (), s32[]{:S(2)}) async-start(), calls=%async_computation.1 | async-start | bytes 4792320 | tf_op jit(solution)/shard_map/reduce_scatter | solution.py:29
  20.3 0.7 copy-start.1
  20.3 1.4 copy-start
Sparse Core Ops, SparseCore 0:
  20.5 815.4 reduce-scatter.1
where the time goes:
time: 1030 us
  waiting for transfers between devices  814 us (79%)
  blocking collectives  187 us (18%)
  between operations  14.1 us (1%)
  matrix products  11.4 us (1%)
    reduce_scatter x1, waiting for transfers between devices, local(): lax.psum_scatter(-jnp.einsum('zh,vzo->hvo', pair_density_matrices, scaled...  814 us
    psum x1, blocking collectives, local(): sigma_diag = lax.psum(partial_contribution, 'pair')  181 us
  transfers between devices with their start and end apart: 1, of which 1 were waited for; matrix products, arithmetic and copies ran while one was open for 0% of the time, Pallas kernels for 0%

commit v1 on v0

--- a/solution.py
+++ b/solution.py
@@ -2,6 +2,10 @@
 import jax.numpy as jnp
 from jax import lax
 from jax.sharding import PartitionSpec as P
+
+
+def make_local_data_for(s0):
+    return lax.all_gather(s0, "pair").sum(axis=0)
 
 
 def pair_weights(energy_bins, bin_weights, pair_total):
@@ -49,7 +53,7 @@
     )
     own_states = lax.dynamic_slice_in_dim(states_wide, pair_position * row_count, row_count, 0)
     partial_contribution = jnp.sum(own_states[:, None, :] * applied, axis=0) / jnp.float32(width)
-    sigma_diag = lax.psum(partial_contribution, "pair")
+    sigma_diag = make_local_data_for(partial_contribution)
     return (applied, sigma_diag)
 
 

time: 1030 us -> 941 us (0.914)
  waiting for transfers between devices: 814 us -> 711 us
  local copies, waits for them, and re-layouts: 2.11 us -> 13.6 us
    reduce_scatter x1 -> x0, waiting for transfers between devices: 814 us -> none  [local(): lax.psum_scatter(-jnp.einsum('zh,vzo->hvo', pair_density_matrices, scaled...]
    unnamed x1 -> x2, waiting for transfers between devices: 0.02 us -> 711 us
    all_gather x0 -> x1, blocking collectives: none -> 181 us  [make_local_data_for(): return lax.all_gather(s0, 'pair').sum(axis=0)]
    psum x1 -> x0, blocking collectives: 181 us -> none  [local(): sigma_diag = lax.psum(partial_contribution, 'pair')]
where the time goes in v1:
time: 941 us
  waiting for transfers between devices  711 us (76%)
  blocking collectives  187 us (20%)
  between operations  14.8 us (2%)
  local copies, waits for them, and re-layouts  13.6 us (1%)
  matrix products  10.8 us (1%)
    unnamed x2, waiting for transfers between devices  711 us
    all_gather x1, blocking collectives, make_local_data_for(): return lax.all_gather(s0, 'pair').sum(axis=0)  181 us
  transfers between devices with their start and end apart: 1, of which 1 were waited for; matrix products, arithmetic and copies ran while one was open for 0% of the time, Pallas kernels for 0%

profile of v1, /device:TPU:2, one launch (start us, length us, event | category | flops | bytes accessed | tf_op | source)
XLA Modules:
  0.0 940.7 jit_solution(4306599785058071764)
XLA Ops:
  7.2 0.0 all-reduce.3.cloned.1.call-start
  7.2 0.0 copy-start.1
  7.2 0.0 copy-start.3
  7.2 1.6 dynamic-slice_convert_fusion
  8.9 2.3 copy.16
  11.2 0.0 copy-done.1
  11.2 0.0 copy-done.3
  11.2 0.3 select_reduce_fusion
  11.5 9.9 %negate_bitcast_fusion = f32[1536,2,384]{0,2,1:T(8,128)} fusion(bf16[2048,1536]{1,0:T(8,128)(2,1)} %param.5, f32[2048,384]{0,1:T(8,128)} %copy.16, f32[2,2048]{1,0:T(2,128)S(1)} %multiply_bitcast_fusion), kind=kOutput, calls=%fused_computation.3 | convolution fusion | flops 4836163584 | bytes 14172160 | tf_op jit(solution)/shard_map/zh,vzo->hvo/dot_general | solution.py:34
  21.4 8.2 copy.17
  29.6 0.0 copy-start.2
  29.6 0.0 copy-start.4
  29.6 0.0 copy-start
  29.6 0.0 all-reduce.3.cloned.1.call-update
  29.6 0.7 copy-done.2
  30.3 0.1 dynamic_slice.14
  30.4 0.1 dynamic_slice.12
  30.4 0.0 copy-done.4
  30.4 0.6 dynamic-slice
  31.7 0.0 copy-done
  31.7 711.5 %all-reduce.3.cloned.1.call-done = f32[1536,2,384]{2,1,0:T(2,128)} async-done(((f32[1536,2,384]{2,1,0:T(2,128)}), f32[1536,2,384]{2,1,0:T(2,128)}) %all-reduce.3.cloned.1.call-update) | async-done | bytes 4718608
  743.2 0.9 constant_dynamic-slice_fusion
  744.1 0.1 fusion.8
  744.2 5.9 all_gather.7
  750.0 0.9 multiply_reduce_fusion
  751.0 181.4 %all-gather.1 = f32[64,2,512]{2,1,0:T(2,128)S(1)} all-gather(f32[1,2,512]{2,1,0:T(2,128)S(1)} %multiply_bitcast_fusion.1), channel_id=2, replica_groups=mesh['pair'=64,'sigma'=4] {'pair'}, dimensions={0}, use_global_device_ids=true | all-gather | bytes 266240 | tf_op jit(solution)/shard_map/all_gather | solution.py:8
  932.4 0.7 copy.19
  933.1 0.7 reduce_sum.29
  (4 shorter events, 0.0 us)
Async XLA Ops:
  7.2 736.0 %all-reduce.3.cloned.1.call-start = ((), (), s32[]{:S(2)}) async-start(), calls=%async_computation | async-start | bytes 9437184
  7.2 4.0 copy-start.1
  7.2 4.0 copy-start.3
  29.6 0.7 copy-start.2
  29.6 0.9 copy-start.4
  29.6 2.1 copy-start
Sparse Core Ops, SparseCore 0:
  29.7 713.4 all-reduce.2
